TPU v7x, 32 devices: a whole 2x2x4 slice. The times are simulated.
32 devices in a mesh: col: 8 (over y, x, core), row: 4 (over z).
Axes of the slice: x: 2, y: 2, z: 4, core: 2. Of those that a mesh axis runs over, the one named last changes fastest.
Arguments:
- w_tiles: bfloat16 [32, 512, 512], P(('col', 'row')), may hold values from -0.09375 to 0.09375
- task_ab: int32 [32], P(('col', 'row')), may hold values from 0 to 3, as said below
- task_ef: int32 [32], P(('col', 'row')), may hold values from 0 to 7
- lam_pairs: bfloat16 [16384, 4096], P('row', 'col'), may hold values from -6 to 6
- other_terms: bfloat16 [2048, 4096], P('row', 'col'), may hold values from -6 to 6
- vir_pair: float32 [2048], P('row'), may hold values from 1 to 4
- occ_pair: float32 [4096], P('col'), may hold values from -3 to -1
Outputs:
- lam_new: bfloat16 [2048, 4096], P('row', 'col')
Inputs may be any that keep to these rules, and one draw needn't show every extreme that they name: Within one row group no pair (task_ab, task_ef) is listed twice.
All inputs are finite; a program needn't handle non-finite values.
Results may differ from a plain program's by a relative error of at most 0.001.
Values may be sent and summed in bfloat16 or wider, within the bound.
No kernel may reach another device: no remote copies, remote signals or barrier semaphores. Data moves between devices by JAX's collectives and lax.ppermute only.
A program may use at most 64 MiB of HBM per device.

v0:
```python
import jax
import jax.numpy as jnp
from jax import lax
from jax.sharding import PartitionSpec as P

AB_T = 4


def add_tile(totals, tile_now, ab_id, ef_id, lam_blocks):
    block = lax.dynamic_index_in_dim(lam_blocks, ef_id, 0, keepdims=False)
    product = jnp.dot(tile_now, block, preferred_element_type=jnp.float32)
    current = lax.dynamic_index_in_dim(totals, ab_id, 0, keepdims=True)
    return lax.dynamic_update_index_in_dim(totals, current + product[None], ab_id, 0)


def body(w_tiles, task_ab, task_ef, lam_pairs, other_terms, vir_pair, occ_pair):
    tile_rows = w_tiles.shape[1]
    col_width = lam_pairs.shape[1]
    ef_count = lam_pairs.shape[0] // tile_rows
    lam_blocks = lam_pairs.reshape(ef_count, tile_rows, col_width)
    all_ab, all_ef = (
        lax.all_gather(task_ab, "col", axis=0, tiled=True),
        lax.all_gather(task_ef, "col", axis=0, tiled=True),
    )
    initial = jnp.zeros((AB_T, tile_rows, col_width), jnp.float32)
    totals = initial
    piece = lax.all_gather(w_tiles, "col", axis=0, tiled=True)
    piece_count = piece.shape[0]
    full_blocks = piece_count // 4

    def block_turn(turn, running):
        base = turn * 4
        tiles_here = lax.dynamic_slice_in_dim(piece, base, 4, 0)
        ab_here = lax.dynamic_slice_in_dim(all_ab, base, 4)
        ef_here = lax.dynamic_slice_in_dim(all_ef, base, 4)
        for inner in range(4):
            running = add_tile(
                running, tiles_here[inner], ab_here[inner], ef_here[inner], lam_blocks
            )
        return running

    totals = lax.fori_loop(0, full_blocks, block_turn, totals)
    ladder = totals
    ladder = ladder.reshape(AB_T * tile_rows, col_width)
    owned = lax.psum_scatter(ladder, "row", scatter_dimension=0, tiled=True)
    combined = other_terms.astype(jnp.float32) + owned
    denominator = occ_pair[None, :] - vir_pair[:, None]
    return (combined / denominator).astype(jnp.bfloat16)


def solution(mesh):
    placed = (
        P(("col", "row"), None, None),
        P(("col", "row")),
        P(("col", "row")),
        P("row", "col"),
        P("row", "col"),
        P("row"),
        P("col"),
    )
    return jax.shard_map(
        body, mesh=mesh, in_specs=placed, out_specs=P("row", "col"), check_vma=False
    )
```

profile of v0, /device:TPU:0, one launch (start us, length us, event | category | flops | bytes accessed | tf_op | source)
XLA Modules:
  0.0 194.1 jit_solution(14418311081692855972)
XLA Ops:
  6.5 0.0 all-gather.2.cloned.1.call-start
  6.5 0.7 all-gather.2.cloned.1.call-update
  7.3 0.0 reduce-scatter.2.cloned.1.call-start
  8.6 1.3 dynamic-slice
  9.9 0.7 dynamic-update-slice
  10.6 0.7 dynamic-update-slice.1
  11.3 9.5 %all-reduce.2 = (s32[8]{0:T(128)S(1)}, s32[8]{0:T(128)S(1)}) all-reduce(s32[8]{0:T(128)S(1)} %dynamic-update-slice, s32[8]{0:T(128)S(1)} %dynamic-update-slice.1), channel_id=1, replica_groups=mesh['col'=8,'row'=4] {'col'}, use_global_device_ids=true, to_apply=%add | all-reduce | flops 16 | bytes 128
  20.8 27.8 %all-gather.2.cloned.1.call-done = bf16[8,512,512]{2,1,0:T(8,128)(2,1)} async-done(((bf16[1,512,512]{2,1,0:T(8,128)(2,1)}), bf16[8,512,512]{2,1,0:T(8,128)(2,1)}) %all-gather.2.cloned.1.call-update) | async-done | bytes 4194320 | tf_op jit(solution)/shard_map/all_gather | solution.py:27
  48.6 2.5 %broadcast_in_dim.33 = f32[4,512,512]{2,1,0:T(8,128)} broadcast(f32[]{:T(128)} %constant.61.clone.1), dimensions={} | broadcast | bytes 4194308 | tf_op jit(solution)/shard_map/broadcast_in_dim | solution.py:25
  51.1 56.9 %while.13 = (s32[]{:T(128)}, f32[4,512,512]{2,1,0:T(8,128)}, s32[8]{0:T(128)S(1)}, bf16[8,512,512]{2,1,0:T(8,128)(2,1)}, s32[8]{0:T(128)S(1)}, /*index=5*/bf16[8...) while((s32[]{:T(128)}, f32[4,512,512]{2,1,0:T(8,128)}, ...), condition=%wide.region_1.2_spmd, body=%wide.region_0.1_spmd.sunk | while | flops 1074790400 | bytes 12583575 | solution.py:42
  51.1 0.1 dynamic_slice.118
  51.2 0.7 fusion.37
  53.7 0.1 dynamic_slice.117
  53.8 0.7 fusion.36
  56.2 3.0 %fusion.38 = f32[4,512,512]{2,1,0:T(8,128)} fusion(f32[4,512,512]{2,1,0:T(8,128)} %get-tuple-element.204, s32[]{:T(128)S(6)} %select_n.82, bf16[8,512,512]{2,1,0:T(8,128)(2,1)} %get-tuple-element.219, s32[]{:T(128)S(6)} %select_n.81, bf16[8,512,512]{2,1,0:T(8,128)(2,1)} %get-tuple-element.221, s32[]{:T(128)S(6)} %select_n.83), kind=kOutput, calls=%fused_computation.5.clone.1 | convolution fusion | flops 268697600 | bytes 3145740 | tf_op jit(solution)/shard_map/while/body/eval_jaxpr/dot_general | solution.py:11
  62.7 3.0 %fusion.39 = f32[4,512,512]{2,1,0:T(8,128)} fusion(f32[4,512,512]{2,1,0:T(8,128)} %fusion.38, s32[]{:T(128)S(6)} %select_n.84, bf16[8,512,512]{2,1,0:T(8,128)(2,1)} %get-tuple-element.219, s32[]{:T(128)S(6)} %add.168, bf16[8,512,512]{2,1,0:T(8,128)(2,1)} %get-tuple-element.221, s32[]{:T(128)S(6)} %select_n.85), kind=kOutput, calls=%fused_computation.7.clone.1 | convolution fusion | flops 268697600 | bytes 3145740 | tf_op jit(solution)/shard_map/while/body/eval_jaxpr/dot_general | solution.py:11
  69.8 3.0 %fusion.40 = f32[4,512,512]{2,1,0:T(8,128)} fusion(f32[4,512,512]{2,1,0:T(8,128)} %fusion.39, s32[]{:T(128)S(6)} %select_n.86, bf16[8,512,512]{2,1,0:T(8,128)(2,1)} %get-tuple-element.219, s32[]{:T(128)S(6)} %add.171, bf16[8,512,512]{2,1,0:T(8,128)(2,1)} %get-tuple-element.221, s32[]{:T(128)S(6)} %select_n.87), kind=kOutput, calls=%fused_computation.9.clone.1 | convolution fusion | flops 268697600 | bytes 3145740 | tf_op jit(solution)/shard_map/while/body/eval_jaxpr/dot_general | solution.py:11
  76.6 3.0 %fusion.41 = f32[4,512,512]{2,1,0:T(8,128)} fusion(f32[4,512,512]{2,1,0:T(8,128)} %fusion.40, s32[]{:T(128)S(6)} %select_n.88, bf16[8,512,512]{2,1,0:T(8,128)(2,1)} %get-tuple-element.219, s32[]{:T(128)S(6)} %add.174, bf16[8,512,512]{2,1,0:T(8,128)(2,1)} %get-tuple-element.221, s32[]{:T(128)S(6)} %select_n.89), kind=kOutput, calls=%fused_computation.11.clone.1 | convolution fusion | flops 268697600 | bytes 3145740 | tf_op jit(solution)/shard_map/while/body/eval_jaxpr/dot_general | solution.py:11
  79.6 0.1 dynamic_slice.118
  79.6 0.7 fusion.37
  82.2 0.1 dynamic_slice.117
  82.2 0.7 fusion.36
  84.6 3.0 %fusion.38 = f32[4,512,512]{2,1,0:T(8,128)} fusion(f32[4,512,512]{2,1,0:T(8,128)} %get-tuple-element.204, s32[]{:T(128)S(6)} %select_n.82, bf16[8,512,512]{2,1,0:T(8,128)(2,1)} %get-tuple-element.219, s32[]{:T(128)S(6)} %select_n.81, bf16[8,512,512]{2,1,0:T(8,128)(2,1)} %get-tuple-element.221, s32[]{:T(128)S(6)} %select_n.83), kind=kOutput, calls=%fused_computation.5.clone.1 | convolution fusion | flops 268697600 | bytes 3145740 | tf_op jit(solution)/shard_map/while/body/eval_jaxpr/dot_general | solution.py:11
  91.2 3.0 %fusion.39 = f32[4,512,512]{2,1,0:T(8,128)} fusion(f32[4,512,512]{2,1,0:T(8,128)} %fusion.38, s32[]{:T(128)S(6)} %select_n.84, bf16[8,512,512]{2,1,0:T(8,128)(2,1)} %get-tuple-element.219, s32[]{:T(128)S(6)} %add.168, bf16[8,512,512]{2,1,0:T(8,128)(2,1)} %get-tuple-element.221, s32[]{:T(128)S(6)} %select_n.85), kind=kOutput, calls=%fused_computation.7.clone.1 | convolution fusion | flops 268697600 | bytes 3145740 | tf_op jit(solution)/shard_map/while/body/eval_jaxpr/dot_general | solution.py:11
  98.3 3.0 %fusion.40 = f32[4,512,512]{2,1,0:T(8,128)} fusion(f32[4,512,512]{2,1,0:T(8,128)} %fusion.39, s32[]{:T(128)S(6)} %select_n.86, bf16[8,512,512]{2,1,0:T(8,128)(2,1)} %get-tuple-element.219, s32[]{:T(128)S(6)} %add.171, bf16[8,512,512]{2,1,0:T(8,128)(2,1)} %get-tuple-element.221, s32[]{:T(128)S(6)} %select_n.87), kind=kOutput, calls=%fused_computation.9.clone.1 | convolution fusion | flops 268697600 | bytes 3145740 | tf_op jit(solution)/shard_map/while/body/eval_jaxpr/dot_general | solution.py:11
  105.0 3.0 %fusion.41 = f32[4,512,512]{2,1,0:T(8,128)} fusion(f32[4,512,512]{2,1,0:T(8,128)} %fusion.40, s32[]{:T(128)S(6)} %select_n.88, bf16[8,512,512]{2,1,0:T(8,128)(2,1)} %get-tuple-element.219, s32[]{:T(128)S(6)} %add.174, bf16[8,512,512]{2,1,0:T(8,128)(2,1)} %get-tuple-element.221, s32[]{:T(128)S(6)} %select_n.89), kind=kOutput, calls=%fused_computation.11.clone.1 | convolution fusion | flops 268697600 | bytes 3145740 | tf_op jit(solution)/shard_map/while/body/eval_jaxpr/dot_general | solution.py:11
  108.0 0.0 reduce-scatter.2.cloned.1.call-update
  108.0 77.0 %reduce-scatter.2.cloned.1.call-done = f32[512,512]{1,0:T(8,128)} async-done(((f32[2048,512]{1,0:T(8,128)}), f32[512,512]{1,0:T(8,128)}) %reduce-scatter.2.cloned.1.call-update) | async-done | bytes 1048592 | tf_op jit(solution)/shard_map/reduce_scatter | solution.py:45
  185.0 0.0 copy-done
  185.0 0.0 copy-done.1
  185.0 0.0 copy-done.2
  185.0 2.3 %divide_convert_fusion = bf16[512,512]{1,0:T(8,128)(2,1)} fusion(f32[512,512]{1,0:T(8,128)} %reduce-scatter.2.cloned.1.call-done, bf16[512,512]{1,0:T(8,128)(2,1)S(1)} %copy-done, f32[512]{0:T(512)S(1)} %copy-done.1, f32[512]{0:T(512)S(1)} %copy-done.2), kind=kLoop, calls=%fused_computation.28 | loop fusion | flops 1310720 | bytes 2101248 | tf_op jit(solution)/shard_map/convert_element_type | solution.py:48
  (5 shorter events, 0.0 us)
Async XLA Ops:
  6.5 42.1 %all-gather.2.cloned.1.call-start = ((), (), s32[]{:S(2)}) async-start(), calls=%async_computation.1 | async-start | bytes 4718592 | tf_op jit(solution)/shard_map/all_gather | solution.py:27
  7.3 177.7 %reduce-scatter.2.cloned.1.call-start = ((), (), s32[]{:S(2)}) async-start(), calls=%async_computation.2 | async-start | bytes 5242880 | tf_op jit(solution)/shard_map/reduce_scatter | solution.py:45
  108.0 77.0 %copy-start = (bf16[512,512]{1,0:T(8,128)(2,1)S(1)}, bf16[512,512]{1,0:T(8,128)(2,1)}, u32[]{:S(2)}) copy-start(bf16[512,512]{1,0:T(8,128)(2,1)} %param.13) | copy-start | bytes 1572868
  108.0 77.0 %copy-start.1 = (f32[512]{0:T(512)S(1)}, f32[512]{0:T(512)}, u32[]{:S(2)}) copy-start(f32[512]{0:T(512)} %param.14) | copy-start | bytes 6148
  108.0 77.0 %copy-start.2 = (f32[512]{0:T(512)S(1)}, f32[512]{0:T(512)}, u32[]{:S(2)}) copy-start(f32[512]{0:T(512)} %param.15) | copy-start | bytes 6148
Sparse Core Ops, SparseCore 0:
  9.2 39.3 all-gather.1
  108.2 76.7 reduce-scatter.1
where the time goes:
time: 195 us; the launch traced here: 194 us
  waiting for transfers between devices  106 us (54%)
  loops' own time  30 us (15%)
  matrix products  23.9 us (12%)
  between operations  14.7 us (8%)
  blocking collectives  9.49 us (5%)
  local copies, waits for them, and re-layouts  8.18 us (4%)
  other arithmetic  2.27 us (1%)
    reduce_scatter x1, waiting for transfers between devices, body(): owned = lax.psum_scatter(ladder, 'row', scatter_dimension=0, tiled=True)  77 us
    another operation x1, loops' own time, body(): totals = lax.fori_loop(0, full_blocks, block_turn, totals)  30 us
    all_gather x1, waiting for transfers between devices, body(): piece = lax.all_gather(w_tiles, 'col', axis=0, tiled=True)  27.8 us
    dot_general x8, matrix products, add_tile(): product = jnp.dot(tile_now, block, preferred_element_type=jnp.float32)  23.9 us
    unnamed x1, blocking collectives  9.49 us
  transfers between devices with their start and end apart: 2, of which 2 were waited for; matrix products, arithmetic and copies ran while one was open for 1% of the time, Pallas kernels for 0%

commit v1 on v0

v1 whole, which is shorter than its diff:
```python
import functools

import jax
import jax.numpy as jnp
from jax import lax
from jax.experimental import pallas as pl
from jax.experimental.pallas import tpu as pltpu
from jax.sharding import PartitionSpec as P

SPLIT = (0.25, 0.625)
HEAD = 8


def chunk_bounds(rows):
    cuts = [0] + [max(16, int(rows * s) // 16 * 16) for s in SPLIT] + [rows]
    return [(a, b) for a, b in zip(cuts[:-1], cuts[1:]) if b > a]


def ladder_kernel(count, row_count, offset, *refs):
    pieces, heads = refs[:count], refs[count : 2 * count]
    lam = refs[2 * count]
    outs = refs[2 * count + 1 : 2 * count + 1 + row_count]
    buf, totals, sems = refs[2 * count + 1 + row_count :]
    depth = buf.shape[1]
    ef_count = lam.shape[0] // depth
    height = pieces[0].shape[0] - offset
    codes, copies = [], []
    for t in range(count):
        code = jnp.max(heads[t][...].astype(jnp.float32)).astype(jnp.int32)
        ef = code % ef_count
        codes.append(code // ef_count)
        copy = pltpu.make_async_copy(
            lam.at[pl.ds(pl.multiple_of(ef * depth, depth), depth), :], buf.at[t], sems.at[t]
        )
        copy.start()
        copies.append(copy)
    totals[...] = jnp.zeros_like(totals)
    for t in range(count):
        copies[t].wait()
        product = jnp.dot(
            pieces[t][pl.ds(offset, height), :], buf[t], preferred_element_type=jnp.float32
        )
        rows = pl.ds(pl.multiple_of(codes[t] * height, height), height)
        totals[rows, :] += product
    me = lax.axis_index("row")
    own = totals.shape[0] // row_count
    for j in range(row_count):
        other = lax.bitwise_xor(me, j)
        outs[j][...] = totals[pl.ds(pl.multiple_of(other * own, own), own), :]


def ladder_chunk(pieces, heads, lam, row_count, ab_tiles, depth, offset):
    count = len(pieces)
    height = pieces[0].shape[0] - offset
    width = lam.shape[1]
    own = ab_tiles * height // row_count
    vmem = pl.BlockSpec(memory_space=pltpu.VMEM)
    head_spec = pl.BlockSpec((HEAD, heads[0].shape[1]), lambda i: (0, 0))
    flops = 2 * count * height * depth * width
    return pl.pallas_call(
        functools.partial(ladder_kernel, count, row_count, offset),
        grid=(1,),
        out_shape=[jax.ShapeDtypeStruct((own, width), jnp.float32)] * row_count,
        in_specs=[vmem] * count + [head_spec] * count + [pl.BlockSpec(memory_space=pl.ANY)],
        out_specs=[vmem] * row_count,
        scratch_shapes=[
            pltpu.VMEM((count, depth, width), lam.dtype),
            pltpu.VMEM((ab_tiles * height, width), jnp.float32),
            pltpu.SemaphoreType.DMA((count,)),
        ],
        compiler_params=pltpu.CompilerParams(vmem_limit_bytes=36 * 2**20),
        cost_estimate=pl.CostEstimate(
            flops=flops, bytes_accessed=count * depth * width * 2, transcendentals=0
        ),
    )(*pieces, *heads, lam)


def body(row_count, col_count, w_tiles, task_ab, task_ef, lam, other, vir, occ):
    tasks, tile_rows, depth = w_tiles.shape
    own_rows = other.shape[0]
    ab_tiles = own_rows * row_count // tile_rows
    sub = tile_rows // own_rows
    ef_count = lam.shape[0] // depth

    def send(x, axis, count, k):
        return lax.ppermute(x, axis, [(i, i ^ k) for i in range(count)])

    bounds = chunk_bounds(own_rows)
    code = (task_ab * ef_count + task_ef).astype(jnp.bfloat16)
    w_rows = w_tiles.reshape(tasks, sub, own_rows, depth)
    bases = []
    for index, (a, b) in enumerate(bounds):
        for t in range(tasks):
            part = w_rows[t, :, a:b].reshape(sub * (b - a), depth)
            if index == 0:
                part = jnp.concatenate([jnp.broadcast_to(code[t], (HEAD, depth)), part], 0)
            bases.append((index, part))
    gathered = {}
    for index, part in bases:
        near = [part] + [send(part, "col", col_count, k) for k in range(2, col_count, 2)]
        gathered.setdefault(index, []).extend(near)
    partial = []
    heads = None
    for index, (a, b) in enumerate(bounds):
        near = gathered[index]
        pieces = near + [send(x, "col", col_count, 1) for x in near]
        heads = pieces if index == 0 else heads
        partial.append(
            ladder_chunk(
                pieces, heads, lam, row_count, ab_tiles, depth, HEAD if index == 0 else 0
            )
        )
    results = []
    for index, (a, b) in enumerate(bounds):
        blocks = partial[index]
        step = 1
        while step < row_count:
            away = jnp.stack([x.astype(jnp.float16) for x in blocks[1::2]])
            here = send(away, "row", row_count, step)
            blocks = [x + here[i].astype(jnp.float32) for i, x in enumerate(blocks[0::2])]
            step *= 2
        combined = other[a:b].astype(jnp.float32) + blocks[0]
        denominator = occ[None, :] - vir[a:b, None]
        results.append((combined / denominator).astype(jnp.bfloat16))
    return jnp.concatenate(results, 0)


def solution(mesh):
    placed = (
        P(("col", "row"), None, None),
        P(("col", "row")),
        P(("col", "row")),
        P("row", "col"),
        P("row", "col"),
        P("row"),
        P("col"),
    )
    return jax.shard_map(
        functools.partial(body, mesh.shape["row"], mesh.shape["col"]),
        mesh=mesh,
        in_specs=placed,
        out_specs=P("row", "col"),
        check_vma=False,
    )
```

time: 195 us -> 82.1 us (0.42)
  waiting for transfers between devices: 106 us -> 40.5 us
  loops' own time: 30 us -> 0 us
  matrix products: 23.9 us -> 0 us
  starting transfers between devices: 0.04 us -> 22.3 us
  between operations: 14.7 us -> 1.49 us
  Pallas kernels: 0 us -> 10.9 us
  blocking collectives: 9.49 us -> 0 us
  local copies, waits for them, and re-layouts: 8.18 us -> 5.01 us
    reduce_scatter x1 -> x0, waiting for transfers between devices: 77 us -> none  [body(): owned = lax.psum_scatter(ladder, 'row', scatter_dimension=0, tiled=True)]
    ppermute x0 -> x27, waiting for transfers between devices: none -> 40.5 us  [send(): return lax.ppermute(x, axis, [(i, i ^ k) for i in range(count)])]
    another operation x1 -> x0, loops' own time: 30 us -> none  [body(): totals = lax.fori_loop(0, full_blocks, block_turn, totals)]
    all_gather x1 -> x0, waiting for transfers between devices: 27.8 us -> none  [body(): piece = lax.all_gather(w_tiles, 'col', axis=0, tiled=True)]
    dot_general x8 -> x0, matrix products: 23.9 us -> none  [add_tile(): product = jnp.dot(tile_now, block, preferred_element_type=jnp.float32)]
    ppermute x0 -> x27, starting transfers between devices: none -> 22.3 us  [send(): return lax.ppermute(x, axis, [(i, i ^ k) for i in range(count)])]
    pallas_call x0 -> x3, Pallas kernels: none -> 10.9 us  [ladder_chunk(): pl.pallas_call(functools.partial(ladder_kernel, count, row_count, offset)...]
    unnamed x1 -> x0, blocking collectives: 9.49 us -> none
  transfers between devices with their start and end apart: 2 -> 27, of which waited for: 2 -> 7; matrix products, arithmetic and copies ran while one was open for 1% -> 3% of each run, Pallas kernels for 0% -> 13%
where the time goes in v1:
time: 82.1 us; the launch traced here: 81.9 us
  waiting for transfers between devices  40.5 us (49%)
  starting transfers between devices  22.3 us (27%)
  Pallas kernels  10.9 us (13%)
  local copies, waits for them, and re-layouts  5.01 us (6%)
  other arithmetic  1.75 us (2%)
  between operations  1.49 us (2%)
    ppermute x27, waiting for transfers between devices, send(): return lax.ppermute(x, axis, [(i, i ^ k) for i in range(count)])  40.5 us
    ppermute x27, starting transfers between devices, send(): return lax.ppermute(x, axis, [(i, i ^ k) for i in range(count)])  22.3 us
    pallas_call x3, Pallas kernels, ladder_chunk(): pl.pallas_call(functools.partial(ladder_kernel, count, row_count, offset)...  10.9 us
    unnamed x8, local copies, waits for them, and re-layouts  2.2 us
    another operation x2, local copies, waits for them, and re-layouts, body(): part = w_rows[t, :, a:b].reshape(sub * (b - a), depth)  1.96 us
  transfers between devices with their start and end apart: 27, of which 7 were waited for; matrix products, arithmetic and copies ran while one was open for 3% of the time, Pallas kernels for 13%

profile of v1, /device:TPU:0, one launch (start us, length us, event | category | flops | bytes accessed | tf_op | source)
XLA Modules:
  0.0 81.9 jit_solution(588361778875366997)
XLA Ops:
  0.0 0.9 %slice_bitcast_fusion.8 = bf16[128,512]{1,0:T(8,128)(2,1)S(1)} fusion(bf16[1,1,512,512]{3,2,1,0:T(8,128)(2,1)} %bitcast.65), kind=kLoop, calls=%fused_computation.40 | loop fusion | bytes 262144 | tf_op jit(solution)/shard_map/reshape;squeeze | solution.py:94
  2.2 3.0 %collective-permute-start = (bf16[136,512]{1,0:T(8,128)(2,1)S(1)}, bf16[136,512]{1,0:T(8,128)(2,1)S(1)}, u32[]{:S(2)}, u32[]{:S(2)}) collective-permute-start(bf16[136,512]{1,0:T(8,128)(2,1)S(1)} %concatenate.6.refs_0_.refs_8_), channel_id=1, source_target_pairs={{0,8},{4,12},{8,0},{12,4},{16,24},{20,28},{24,16},{28,20},{1,9},{5... | collective-permute-start | bytes 417800 | tf_op jit(solution)/shard_map/ppermute | solution.py:86
  5.3 1.5 %collective-permute-start.1 = (bf16[136,512]{1,0:T(8,128)(2,1)S(1)}, bf16[136,512]{1,0:T(8,128)(2,1)S(1)}, u32[]{:S(2)}, u32[]{:S(2)}) collective-permute-start(bf16[136,512]{1,0:T(8,128)(2,1)S(1)} %concatenate.6.refs_0_.refs_8_), channel_id=1, source_target_pairs={{0,16},{4,20},{8,24},{12,28},{16,0},{20,4},{24,8},{28,12},{1,17},{... | collective-permute-start | bytes 417800 | tf_op jit(solution)/shard_map/ppermute | solution.py:86
  6.8 2.5 %collective-permute-done.refs_1_.refs_9_ = bf16[136,512]{1,0:T(8,128)(2,1)S(1)} collective-permute-done((bf16[136,512]{1,0:T(8,128)(2,1)S(1)}, bf16[136,512]{1,0:T(8,128)(2,1)S(1)}, u32[]{:S(2)}, u32[]{:S(2)}) %collective-permute-start) | collective-permute-done | bytes 139296 | tf_op jit(solution)/shard_map/ppermute | solution.py:86
  9.3 4.1 %collective-permute-done.1.refs_2_.refs_10_ = bf16[136,512]{1,0:T(8,128)(2,1)S(1)} collective-permute-done((bf16[136,512]{1,0:T(8,128)(2,1)S(1)}, bf16[136,512]{1,0:T(8,128)(2,1)S(1)}, u32[]{:S(2)}, u32[]{:S(2)}) %collective-permute-start.1) | collective-permute-done | bytes 139296 | tf_op jit(solution)/shard_map/ppermute | solution.py:86
  13.4 0.5 collective-permute-start.6
  13.9 1.0 %slice_bitcast_fusion.5 = (bf16[192,512]{1,0:T(8,128)(2,1)S(1)}, bf16[192,512]{1,0:T(8,128)(2,1)S(1)}) fusion(bf16[1,1,512,512]{3,2,1,0:T(8,128)(2,1)} %bitcast.66), kind=kLoop, calls=%fused_computation.32 | loop fusion | bytes 786432 | tf_op jit(solution)/shard_map/reshape;squeeze | solution.py:94
  15.0 0.8 collective-permute-start.9
  15.7 1.3 %collective-permute-start.10 = (bf16[192,512]{1,0:T(8,128)(2,1)S(1)}, bf16[192,512]{1,0:T(8,128)(2,1)S(1)}, u32[]{:S(2)}, u32[]{:S(2)}) collective-permute-start(bf16[192,512]{1,0:T(8,128)(2,1)S(1)} %get-tuple-element.31.refs_0_), channel_id=1, source_target_pairs={{0,16},{4,20},{8,24},{12,28},{16,0},{20,4},{24,8},{28,12},{1,17},{... | collective-permute-start | bytes 589832 | tf_op jit(solution)/shard_map/ppermute | solution.py:86
  17.1 1.4 %collective-permute-start.11 = (bf16[192,512]{1,0:T(8,128)(2,1)S(1)}, bf16[192,512]{1,0:T(8,128)(2,1)S(1)}, u32[]{:S(2)}, u32[]{:S(2)}) collective-permute-start(bf16[192,512]{1,0:T(8,128)(2,1)S(1)} %get-tuple-element.31.refs_0_), channel_id=1, source_target_pairs={{0,24},{4,28},{8,16},{12,20},{16,8},{20,12},{24,0},{28,4},{1,25},{... | collective-permute-start | bytes 589832 | tf_op jit(solution)/shard_map/ppermute | solution.py:86
  18.5 0.8 collective-permute-start.18
  19.3 0.8 %fusion.15 = (f32[192]{0:T(256)S(1)}, f32[192]{0:T(256)S(1)}) fusion(f32[512]{0:T(512)} %param.12), kind=kLoop, calls=%fused_computation.43 | loop fusion | bytes 3072 | tf_op jit(solution)/shard_map/slice | solution.py:123
  20.1 2.2 %copy-done = bf16[4096,512]{1,0:T(8,128)(2,1)S(1)} copy-done((bf16[4096,512]{1,0:T(8,128)(2,1)S(1)}, bf16[4096,512]{1,0:T(8,128)(2,1)}, u32[]{:S(2)}) %copy-start) | copy-done | bytes 4194328
  22.3 3.4 %shard_map.73 = (f32[128,512]{1,0:T(8,128)S(1)}, f32[128,512]{1,0:T(8,128)S(1)}, f32[128,512]{1,0:T(8,128)S(1)}, f32[128,512]{1,0:T(8,128)S(1)}) custom-call(bf16[136,512]{1,0:T(8,128)(2,1)S(1)} %concatenate.6.refs_0_.refs_8_, bf16[136,512]{1,0:T(8,128)(2,1)S(1)} %collective-permute-done.refs_1_.refs_9_, ...), custom_call_target="tpu_custom_call" | custom-call | flops 536870912 | bytes 4194304 | tf_op jit(solution)/shard_map/pallas_call | solution.py:60
  25.7 1.4 %collective-permute-start.19 = (bf16[192,512]{1,0:T(8,128)(2,1)S(1)}, bf16[192,512]{1,0:T(8,128)(2,1)S(1)}, u32[]{:S(2)}, u32[]{:S(2)}) collective-permute-start(bf16[192,512]{1,0:T(8,128)(2,1)S(1)} %get-tuple-element.32.refs_0_), channel_id=1, source_target_pairs={{0,16},{4,20},{8,24},{12,28},{16,0},{20,4},{24,8},{28,12},{1,17},{... | collective-permute-start | bytes 589832 | tf_op jit(solution)/shard_map/ppermute | solution.py:86
  27.1 1.6 %collective-permute-start.20 = (bf16[192,512]{1,0:T(8,128)(2,1)S(1)}, bf16[192,512]{1,0:T(8,128)(2,1)S(1)}, u32[]{:S(2)}, u32[]{:S(2)}) collective-permute-start(bf16[192,512]{1,0:T(8,128)(2,1)S(1)} %get-tuple-element.32.refs_0_), channel_id=1, source_target_pairs={{0,24},{4,28},{8,16},{12,20},{16,8},{20,12},{24,0},{28,4},{1,25},{... | collective-permute-start | bytes 589832 | tf_op jit(solution)/shard_map/ppermute | solution.py:86
  28.8 0.5 collective-permute-start.14
  29.3 1.6 %collective-permute-done.18.refs_1_ = bf16[192,512]{1,0:T(8,128)(2,1)S(1)} collective-permute-done((bf16[192,512]{1,0:T(8,128)(2,1)S(1)}, bf16[192,512]{1,0:T(8,128)(2,1)S(1)}, u32[]{:S(2)}, u32[]{:S(2)}) %collective-permute-start.18) | collective-permute-done | bytes 196640 | tf_op jit(solution)/shard_map/ppermute | solution.py:86
  31.0 6.0 %collective-permute-done.19.refs_2_ = bf16[192,512]{1,0:T(8,128)(2,1)S(1)} collective-permute-done((bf16[192,512]{1,0:T(8,128)(2,1)S(1)}, bf16[192,512]{1,0:T(8,128)(2,1)S(1)}, u32[]{:S(2)}, u32[]{:S(2)}) %collective-permute-start.19) | collective-permute-done | bytes 196640 | tf_op jit(solution)/shard_map/ppermute | solution.py:86
  37.0 0.5 collective-permute-start.22
  37.6 0.4 collective-permute-start.24
  38.0 1.6 %collective-permute-start.7 = (f16[2,128,512]{2,1,0:T(8,128)(2,1)S(1)}, f16[2,128,512]{2,1,0:T(8,128)(2,1)S(1)}, u32[]{:S(2)}, u32[]{:S(2)}) collective-permute-start(f16[2,128,512]{2,1,0:T(8,128)(2,1)S(1)} %pad_maximum_fusion.3), channel_id=1, source_target_pairs={{0,1},{1,0},{2,3},{3,2},{4,5},{5,4},{6,7},{7,6},{8,9},{9,8},{10,11... | collective-permute-start | bytes 786440 | tf_op jit(solution)/shard_map/ppermute | solution.py:86
  39.6 3.7 %shard_map.74 = (f32[192,512]{1,0:T(8,128)S(1)}, f32[192,512]{1,0:T(8,128)S(1)}, f32[192,512]{1,0:T(8,128)S(1)}, f32[192,512]{1,0:T(8,128)S(1)}) custom-call(bf16[192,512]{1,0:T(8,128)(2,1)S(1)} %get-tuple-element.31.refs_0_, bf16[192,512]{1,0:T(8,128)(2,1)S(1)} %collective-permute-done.9.refs_1_, bf16[192,512]{1,0:T(8,128)(2,1)S(1)} %collective-permute-done.10.refs_2_, ...), custom_call_target="tpu_custom_call" | custom-call | flops 805306368 | bytes 4194304 | tf_op jit(solution)/shard_map/pallas_call | solution.py:60
  43.6 0.5 collective-permute-start.16
  44.1 3.7 %shard_map.75 = (f32[192,512]{1,0:T(8,128)S(1)}, f32[192,512]{1,0:T(8,128)S(1)}, f32[192,512]{1,0:T(8,128)S(1)}, f32[192,512]{1,0:T(8,128)S(1)}) custom-call(bf16[192,512]{1,0:T(8,128)(2,1)S(1)} %get-tuple-element.32.refs_0_, bf16[192,512]{1,0:T(8,128)(2,1)S(1)} %collective-permute-done.18.refs_1_, bf16[192,512]{1,0:T(8,128)(2,1)S(1)} %collective-permute-done.19.refs_2_, ...), custom_call_target="tpu_custom_call" | custom-call | flops 805306368 | bytes 4194304 | tf_op jit(solution)/shard_map/pallas_call | solution.py:60
  48.0 1.6 %collective-permute-start.25 = (f16[2,192,512]{2,1,0:T(8,128)(2,1)S(1)}, f16[2,192,512]{2,1,0:T(8,128)(2,1)S(1)}, u32[]{:S(2)}, u32[]{:S(2)}) collective-permute-start(f16[2,192,512]{2,1,0:T(8,128)(2,1)S(1)} %pad_maximum_fusion.2), channel_id=1, source_target_pairs={{0,1},{1,0},{2,3},{3,2},{4,5},{5,4},{6,7},{7,6},{8,9},{9,8},{10,11... | collective-permute-start | bytes 1179656 | tf_op jit(solution)/shard_map/ppermute | solution.py:86
  49.7 2.7 %collective-permute-start.8 = (f16[1,128,512]{2,1,0:T(8,128)(2,1)S(1)}, f16[1,128,512]{2,1,0:T(8,128)(2,1)S(1)}, u32[]{:S(2)}, u32[]{:S(2)}) collective-permute-start(f16[1,128,512]{2,1,0:T(8,128)(2,1)S(1)} %fusion.14), channel_id=1, source_target_pairs={{0,2},{1,3},{2,0},{3,1},{4,6},{5,7},{6,4},{7,5},{8,10},{9,11},{10,... | collective-permute-start | bytes 393224 | tf_op jit(solution)/shard_map/ppermute | solution.py:86
  52.3 6.1 %collective-permute-done.16 = f16[2,192,512]{2,1,0:T(8,128)(2,1)S(1)} collective-permute-done((f16[2,192,512]{2,1,0:T(8,128)(2,1)S(1)}, f16[2,192,512]{2,1,0:T(8,128)(2,1)S(1)}, u32[]{:S(2)}, u32[]{:S(2)}) %collective-permute-start.16) | collective-permute-done | bytes 393248 | tf_op jit(solution)/shard_map/ppermute | solution.py:86
  58.5 1.8 %collective-permute-start.17 = (f16[1,192,512]{2,1,0:T(8,128)(2,1)S(1)}, f16[1,192,512]{2,1,0:T(8,128)(2,1)S(1)}, u32[]{:S(2)}, u32[]{:S(2)}) collective-permute-start(f16[1,192,512]{2,1,0:T(8,128)(2,1)S(1)} %fusion.12), channel_id=1, source_target_pairs={{0,2},{1,3},{2,0},{3,1},{4,6},{5,7},{6,4},{7,5},{8,10},{9,11},{10,... | collective-permute-start | bytes 589832 | tf_op jit(solution)/shard_map/ppermute | solution.py:86
  60.3 9.9 %collective-permute-done.25 = f16[2,192,512]{2,1,0:T(8,128)(2,1)S(1)} collective-permute-done((f16[2,192,512]{2,1,0:T(8,128)(2,1)S(1)}, f16[2,192,512]{2,1,0:T(8,128)(2,1)S(1)}, u32[]{:S(2)}, u32[]{:S(2)}) %collective-permute-start.25) | collective-permute-done | bytes 393248 | tf_op jit(solution)/shard_map/ppermute | solution.py:86
  70.5 10.3 %collective-permute-done.26 = f16[1,192,512]{2,1,0:T(8,128)(2,1)S(1)} collective-permute-done((f16[1,192,512]{2,1,0:T(8,128)(2,1)S(1)}, f16[1,192,512]{2,1,0:T(8,128)(2,1)S(1)}, u32[]{:S(2)}, u32[]{:S(2)}) %collective-permute-start.26) | collective-permute-done | bytes 196640 | tf_op jit(solution)/shard_map/ppermute | solution.py:86
  81.1 0.8 %pad_maximum_fusion = bf16[512,512]{1,0:T(8,128)(2,1)} fusion(bf16[192,512]{1,0:T(8,128)(2,1)S(1)} %get-tuple-element.30, bf16[192,512]{1,0:T(8,128)(2,1)S(1)} %get-tuple-element.29, bf16[128,512]{1,0:T(8,128)(2,1)S(1)} %fusion.10), kind=kLoop, calls=%fused_computation | loop fusion | flops 1572864 | bytes 1048576 | tf_op jit(solution)/shard_map/concatenate | solution.py:125
  (51 shorter events, 1.3 us)
Async XLA Ops:
  2.2 7.1 %collective-permute-start = (bf16[136,512]{1,0:T(8,128)(2,1)S(1)}, bf16[136,512]{1,0:T(8,128)(2,1)S(1)}, u32[]{:S(2)}, u32[]{:S(2)}) collective-permute-start(bf16[136,512]{1,0:T(8,128)(2,1)S(1)} %concatenate.6.refs_0_.refs_8_), channel_id=1, source_target_pairs={{0,8},{4,12},{8,0},{12,4},{16,24},{20,28},{24,16},{28,20},{1,9},{5... | collective-permute-start | bytes 417800 | tf_op jit(solution)/shard_map/ppermute | solution.py:86
  5.3 8.1 %collective-permute-start.1 = (bf16[136,512]{1,0:T(8,128)(2,1)S(1)}, bf16[136,512]{1,0:T(8,128)(2,1)S(1)}, u32[]{:S(2)}, u32[]{:S(2)}) collective-permute-start(bf16[136,512]{1,0:T(8,128)(2,1)S(1)} %concatenate.6.refs_0_.refs_8_), channel_id=1, source_target_pairs={{0,16},{4,20},{8,24},{12,28},{16,0},{20,4},{24,8},{28,12},{1,17},{... | collective-permute-start | bytes 417800 | tf_op jit(solution)/shard_map/ppermute | solution.py:86
  6.8 6.6 %collective-permute-start.2 = (bf16[136,512]{1,0:T(8,128)(2,1)S(1)}, bf16[136,512]{1,0:T(8,128)(2,1)S(1)}, u32[]{:S(2)}, u32[]{:S(2)}) collective-permute-start(bf16[136,512]{1,0:T(8,128)(2,1)S(1)} %concatenate.6.refs_0_.refs_8_), channel_id=1, source_target_pairs={{0,24},{4,28},{8,16},{12,20},{16,8},{20,12},{24,0},{28,4},{1,25},{... | collective-permute-start | bytes 417800 | tf_op jit(solution)/shard_map/ppermute | solution.py:86
  6.8 8.9 %collective-permute-start.3 = (bf16[136,512]{1,0:T(8,128)(2,1)S(1)}, bf16[136,512]{1,0:T(8,128)(2,1)S(1)}, u32[]{:S(2)}, u32[]{:S(2)}) collective-permute-start(bf16[136,512]{1,0:T(8,128)(2,1)S(1)} %concatenate.6.refs_0_.refs_8_), channel_id=1, source_target_pairs={{0,4},{4,0},{8,12},{12,8},{16,20},{20,16},{24,28},{28,24},{1,5},{5... | collective-permute-start | bytes 417800 | tf_op jit(solution)/shard_map/ppermute | solution.py:86
  9.3 7.7 %collective-permute-start.4 = (bf16[136,512]{1,0:T(8,128)(2,1)S(1)}, bf16[136,512]{1,0:T(8,128)(2,1)S(1)}, u32[]{:S(2)}, u32[]{:S(2)}) collective-permute-start(bf16[136,512]{1,0:T(8,128)(2,1)S(1)} %collective-permute-done.refs_1_.refs_9_), channel_id=1, source_target_pairs={{0,4},{4,0},{8,12},{12,8},{16,20},{20,16},{24,28},{28,24},{1,5},{5... | collective-permute-start | bytes 417800 | tf_op jit(solution)/shard_map/ppermute | solution.py:86
  13.4 5.1 %collective-permute-start.5 = (bf16[136,512]{1,0:T(8,128)(2,1)S(1)}, bf16[136,512]{1,0:T(8,128)(2,1)S(1)}, u32[]{:S(2)}, u32[]{:S(2)}) collective-permute-start(bf16[136,512]{1,0:T(8,128)(2,1)S(1)} %collective-permute-done.1.refs_2_.refs_10_), channel_id=1, source_target_pairs={{0,4},{4,0},{8,12},{12,8},{16,20},{20,16},{24,28},{28,24},{1,5},{5... | collective-permute-start | bytes 417800 | tf_op jit(solution)/shard_map/ppermute | solution.py:86
  13.4 5.1 %collective-permute-start.6 = (bf16[136,512]{1,0:T(8,128)(2,1)S(1)}, bf16[136,512]{1,0:T(8,128)(2,1)S(1)}, u32[]{:S(2)}, u32[]{:S(2)}) collective-permute-start(bf16[136,512]{1,0:T(8,128)(2,1)S(1)} %collective-permute-done.2.refs_3_.refs_11_), channel_id=1, source_target_pairs={{0,4},{4,0},{8,12},{12,8},{16,20},{20,16},{24,28},{28,24},{1,5},{5... | collective-permute-start | bytes 417800 | tf_op jit(solution)/shard_map/ppermute | solution.py:86
  15.0 10.8 %collective-permute-start.9 = (bf16[192,512]{1,0:T(8,128)(2,1)S(1)}, bf16[192,512]{1,0:T(8,128)(2,1)S(1)}, u32[]{:S(2)}, u32[]{:S(2)}) collective-permute-start(bf16[192,512]{1,0:T(8,128)(2,1)S(1)} %get-tuple-element.31.refs_0_), channel_id=1, source_target_pairs={{0,8},{4,12},{8,0},{12,4},{16,24},{20,28},{24,16},{28,20},{1,9},{5... | collective-permute-start | bytes 589832 | tf_op jit(solution)/shard_map/ppermute | solution.py:86
  15.7 11.4 %collective-permute-start.10 = (bf16[192,512]{1,0:T(8,128)(2,1)S(1)}, bf16[192,512]{1,0:T(8,128)(2,1)S(1)}, u32[]{:S(2)}, u32[]{:S(2)}) collective-permute-start(bf16[192,512]{1,0:T(8,128)(2,1)S(1)} %get-tuple-element.31.refs_0_), channel_id=1, source_target_pairs={{0,16},{4,20},{8,24},{12,28},{16,0},{20,4},{24,8},{28,12},{1,17},{... | collective-permute-start | bytes 589832 | tf_op jit(solution)/shard_map/ppermute | solution.py:86
  17.1 11.7 %collective-permute-start.11 = (bf16[192,512]{1,0:T(8,128)(2,1)S(1)}, bf16[192,512]{1,0:T(8,128)(2,1)S(1)}, u32[]{:S(2)}, u32[]{:S(2)}) collective-permute-start(bf16[192,512]{1,0:T(8,128)(2,1)S(1)} %get-tuple-element.31.refs_0_), channel_id=1, source_target_pairs={{0,24},{4,28},{8,16},{12,20},{16,8},{20,12},{24,0},{28,4},{1,25},{... | collective-permute-start | bytes 589832 | tf_op jit(solution)/shard_map/ppermute | solution.py:86
  18.5 10.2 %collective-permute-start.12 = (bf16[192,512]{1,0:T(8,128)(2,1)S(1)}, bf16[192,512]{1,0:T(8,128)(2,1)S(1)}, u32[]{:S(2)}, u32[]{:S(2)}) collective-permute-start(bf16[192,512]{1,0:T(8,128)(2,1)S(1)} %get-tuple-element.31.refs_0_), channel_id=1, source_target_pairs={{0,4},{4,0},{8,12},{12,8},{16,20},{20,16},{24,28},{28,24},{1,5},{5... | collective-permute-start | bytes 589832 | tf_op jit(solution)/shard_map/ppermute | solution.py:86
  18.5 12.3 %collective-permute-start.18 = (bf16[192,512]{1,0:T(8,128)(2,1)S(1)}, bf16[192,512]{1,0:T(8,128)(2,1)S(1)}, u32[]{:S(2)}, u32[]{:S(2)}) collective-permute-start(bf16[192,512]{1,0:T(8,128)(2,1)S(1)} %get-tuple-element.32.refs_0_), channel_id=1, source_target_pairs={{0,8},{4,12},{8,0},{12,4},{16,24},{20,28},{24,16},{28,20},{1,9},{5... | collective-permute-start | bytes 589832 | tf_op jit(solution)/shard_map/ppermute | solution.py:86
  20.1 2.2 %copy-start = (bf16[4096,512]{1,0:T(8,128)(2,1)S(1)}, bf16[4096,512]{1,0:T(8,128)(2,1)}, u32[]{:S(2)}) copy-start(bf16[4096,512]{1,0:T(8,128)(2,1)} %refs_16_.5) | copy-start | bytes 12582916
  22.3 17.3 %copy-start.1 = (bf16[4096,512]{1,0:T(8,128)(2,1)S(1)}, bf16[4096,512]{1,0:T(8,128)(2,1)}, u32[]{:S(2)}) copy-start(bf16[4096,512]{1,0:T(8,128)(2,1)} %refs_16_.5) | copy-start | bytes 12582916
  25.7 11.2 %collective-permute-start.19 = (bf16[192,512]{1,0:T(8,128)(2,1)S(1)}, bf16[192,512]{1,0:T(8,128)(2,1)S(1)}, u32[]{:S(2)}, u32[]{:S(2)}) collective-permute-start(bf16[192,512]{1,0:T(8,128)(2,1)S(1)} %get-tuple-element.32.refs_0_), channel_id=1, source_target_pairs={{0,16},{4,20},{8,24},{12,28},{16,0},{20,4},{24,8},{28,12},{1,17},{... | collective-permute-start | bytes 589832 | tf_op jit(solution)/shard_map/ppermute | solution.py:86
  27.1 9.9 %collective-permute-start.20 = (bf16[192,512]{1,0:T(8,128)(2,1)S(1)}, bf16[192,512]{1,0:T(8,128)(2,1)S(1)}, u32[]{:S(2)}, u32[]{:S(2)}) collective-permute-start(bf16[192,512]{1,0:T(8,128)(2,1)S(1)} %get-tuple-element.32.refs_0_), channel_id=1, source_target_pairs={{0,24},{4,28},{8,16},{12,20},{16,8},{20,12},{24,0},{28,4},{1,25},{... | collective-permute-start | bytes 589832 | tf_op jit(solution)/shard_map/ppermute | solution.py:86
  28.8 8.8 %collective-permute-start.13 = (bf16[192,512]{1,0:T(8,128)(2,1)S(1)}, bf16[192,512]{1,0:T(8,128)(2,1)S(1)}, u32[]{:S(2)}, u32[]{:S(2)}) collective-permute-start(bf16[192,512]{1,0:T(8,128)(2,1)S(1)} %collective-permute-done.9.refs_1_), channel_id=1, source_target_pairs={{0,4},{4,0},{8,12},{12,8},{16,20},{20,16},{24,28},{28,24},{1,5},{5... | collective-permute-start | bytes 589832 | tf_op jit(solution)/shard_map/ppermute | solution.py:86
  28.8 8.8 %collective-permute-start.14 = (bf16[192,512]{1,0:T(8,128)(2,1)S(1)}, bf16[192,512]{1,0:T(8,128)(2,1)S(1)}, u32[]{:S(2)}, u32[]{:S(2)}) collective-permute-start(bf16[192,512]{1,0:T(8,128)(2,1)S(1)} %collective-permute-done.10.refs_2_), channel_id=1, source_target_pairs={{0,4},{4,0},{8,12},{12,8},{16,20},{20,16},{24,28},{28,24},{1,5},{5... | collective-permute-start | bytes 589832 | tf_op jit(solution)/shard_map/ppermute | solution.py:86
  30.8 7.2 %collective-permute-start.15 = (bf16[192,512]{1,0:T(8,128)(2,1)S(1)}, bf16[192,512]{1,0:T(8,128)(2,1)S(1)}, u32[]{:S(2)}, u32[]{:S(2)}) collective-permute-start(bf16[192,512]{1,0:T(8,128)(2,1)S(1)} %collective-permute-done.11.refs_3_), channel_id=1, source_target_pairs={{0,4},{4,0},{8,12},{12,8},{16,20},{20,16},{24,28},{28,24},{1,5},{5... | collective-permute-start | bytes 589832 | tf_op jit(solution)/shard_map/ppermute | solution.py:86
  37.0 6.6 %collective-permute-start.21 = (bf16[192,512]{1,0:T(8,128)(2,1)S(1)}, bf16[192,512]{1,0:T(8,128)(2,1)S(1)}, u32[]{:S(2)}, u32[]{:S(2)}) collective-permute-start(bf16[192,512]{1,0:T(8,128)(2,1)S(1)} %get-tuple-element.32.refs_0_), channel_id=1, source_target_pairs={{0,4},{4,0},{8,12},{12,8},{16,20},{20,16},{24,28},{28,24},{1,5},{5... | collective-permute-start | bytes 589832 | tf_op jit(solution)/shard_map/ppermute | solution.py:86
  37.0 7.1 %collective-permute-start.22 = (bf16[192,512]{1,0:T(8,128)(2,1)S(1)}, bf16[192,512]{1,0:T(8,128)(2,1)S(1)}, u32[]{:S(2)}, u32[]{:S(2)}) collective-permute-start(bf16[192,512]{1,0:T(8,128)(2,1)S(1)} %collective-permute-done.18.refs_1_), channel_id=1, source_target_pairs={{0,4},{4,0},{8,12},{12,8},{16,20},{20,16},{24,28},{28,24},{1,5},{5... | collective-permute-start | bytes 589832 | tf_op jit(solution)/shard_map/ppermute | solution.py:86
  37.5 6.6 %collective-permute-start.23 = (bf16[192,512]{1,0:T(8,128)(2,1)S(1)}, bf16[192,512]{1,0:T(8,128)(2,1)S(1)}, u32[]{:S(2)}, u32[]{:S(2)}) collective-permute-start(bf16[192,512]{1,0:T(8,128)(2,1)S(1)} %collective-permute-done.19.refs_2_), channel_id=1, source_target_pairs={{0,4},{4,0},{8,12},{12,8},{16,20},{20,16},{24,28},{28,24},{1,5},{5... | collective-permute-start | bytes 589832 | tf_op jit(solution)/shard_map/ppermute | solution.py:86
  37.6 6.5 %collective-permute-start.24 = (bf16[192,512]{1,0:T(8,128)(2,1)S(1)}, bf16[192,512]{1,0:T(8,128)(2,1)S(1)}, u32[]{:S(2)}, u32[]{:S(2)}) collective-permute-start(bf16[192,512]{1,0:T(8,128)(2,1)S(1)} %collective-permute-done.20.refs_3_), channel_id=1, source_target_pairs={{0,4},{4,0},{8,12},{12,8},{16,20},{20,16},{24,28},{28,24},{1,5},{5... | collective-permute-start | bytes 589832 | tf_op jit(solution)/shard_map/ppermute | solution.py:86
  38.0 11.6 %collective-permute-start.7 = (f16[2,128,512]{2,1,0:T(8,128)(2,1)S(1)}, f16[2,128,512]{2,1,0:T(8,128)(2,1)S(1)}, u32[]{:S(2)}, u32[]{:S(2)}) collective-permute-start(f16[2,128,512]{2,1,0:T(8,128)(2,1)S(1)} %pad_maximum_fusion.3), channel_id=1, source_target_pairs={{0,1},{1,0},{2,3},{3,2},{4,5},{5,4},{6,7},{7,6},{8,9},{9,8},{10,11... | collective-permute-start | bytes 786440 | tf_op jit(solution)/shard_map/ppermute | solution.py:86
  43.5 26.9 %copy-start.2 = (bf16[512,512]{1,0:T(8,128)(2,1)S(1)}, bf16[512,512]{1,0:T(8,128)(2,1)}, u32[]{:S(2)}) copy-start(bf16[512,512]{1,0:T(8,128)(2,1)} %param.11) | copy-start | bytes 1572868
  43.5 26.9 %copy-start.3 = (f32[512]{0:T(512)S(1)}, f32[512]{0:T(512)}, u32[]{:S(2)}) copy-start(f32[512]{0:T(512)} %param.13) | copy-start | bytes 6148
  43.5 26.9 %slice-start = ((f32[512]{0:T(512)}), f32[128]{0:T(128)S(1)}, s32[]{:S(2)}) async-start(f32[512]{0:T(512)} %param.12), calls=%async_computation | async-start | bytes 1024 | tf_op jit(solution)/shard_map/slice | solution.py:123
  43.6 14.9 %collective-permute-start.16 = (f16[2,192,512]{2,1,0:T(8,128)(2,1)S(1)}, f16[2,192,512]{2,1,0:T(8,128)(2,1)S(1)}, u32[]{:S(2)}, u32[]{:S(2)}) collective-permute-start(f16[2,192,512]{2,1,0:T(8,128)(2,1)S(1)} %pad_maximum_fusion.1), channel_id=1, source_target_pairs={{0,1},{1,0},{2,3},{3,2},{4,5},{5,4},{6,7},{7,6},{8,9},{9,8},{10,11... | collective-permute-start | bytes 1179656 | tf_op jit(solution)/shard_map/ppermute | solution.py:86
  48.0 22.2 %collective-permute-start.25 = (f16[2,192,512]{2,1,0:T(8,128)(2,1)S(1)}, f16[2,192,512]{2,1,0:T(8,128)(2,1)S(1)}, u32[]{:S(2)}, u32[]{:S(2)}) collective-permute-start(f16[2,192,512]{2,1,0:T(8,128)(2,1)S(1)} %pad_maximum_fusion.2), channel_id=1, source_target_pairs={{0,1},{1,0},{2,3},{3,2},{4,5},{5,4},{6,7},{7,6},{8,9},{9,8},{10,11... | collective-permute-start | bytes 1179656 | tf_op jit(solution)/shard_map/ppermute | solution.py:86
  49.7 20.7 %collective-permute-start.8 = (f16[1,128,512]{2,1,0:T(8,128)(2,1)S(1)}, f16[1,128,512]{2,1,0:T(8,128)(2,1)S(1)}, u32[]{:S(2)}, u32[]{:S(2)}) collective-permute-start(f16[1,128,512]{2,1,0:T(8,128)(2,1)S(1)} %fusion.14), channel_id=1, source_target_pairs={{0,2},{1,3},{2,0},{3,1},{4,6},{5,7},{6,4},{7,5},{8,10},{9,11},{10,... | collective-permute-start | bytes 393224 | tf_op jit(solution)/shard_map/ppermute | solution.py:86
  58.5 12.1 %collective-permute-start.17 = (f16[1,192,512]{2,1,0:T(8,128)(2,1)S(1)}, f16[1,192,512]{2,1,0:T(8,128)(2,1)S(1)}, u32[]{:S(2)}, u32[]{:S(2)}) collective-permute-start(f16[1,192,512]{2,1,0:T(8,128)(2,1)S(1)} %fusion.12), channel_id=1, source_target_pairs={{0,2},{1,3},{2,0},{3,1},{4,6},{5,7},{6,4},{7,5},{8,10},{9,11},{10,... | collective-permute-start | bytes 589832 | tf_op jit(solution)/shard_map/ppermute | solution.py:86
  70.2 10.6 %collective-permute-start.26 = (f16[1,192,512]{2,1,0:T(8,128)(2,1)S(1)}, f16[1,192,512]{2,1,0:T(8,128)(2,1)S(1)}, u32[]{:S(2)}, u32[]{:S(2)}) collective-permute-start(f16[1,192,512]{2,1,0:T(8,128)(2,1)S(1)} %fusion.13), channel_id=1, source_target_pairs={{0,2},{1,3},{2,0},{3,1},{4,6},{5,7},{6,4},{7,5},{8,10},{9,11},{10,... | collective-permute-start | bytes 589832 | tf_op jit(solution)/shard_map/ppermute | solution.py:86
